TPU v7x, 128 devices: a whole 4x4x4 slice. The times are simulated.
128 devices in a mesh: pairs: 4 (over y_hi, core), stripe: 32 (over z, y_lo, x).
Axes of the slice: x: 4, y: 4 (y_hi: 2, y_lo: 2; y = y_hi * 2 + y_lo), z: 4, core: 2. Of those that a mesh axis runs over, the one named last changes fastest.
Arguments:
- slc_stack: bfloat16 [256, 2, 128, 4096], P(('pairs', 'stripe')), may hold values from -16 to 16
- az_offset: int32 [256], replicated, may hold values from -8 to 8
- rg_offset: int32 [256], replicated, may hold values from -16 to 16
- pair_list: int32 [1000, 2], replicated, may hold values from 0 to 255, as said below
Outputs:
- screen: float32 [256, 2, 32, 256], P(None, None, 'pairs', 'stripe')
- motion: float32 [256, 2, 32, 256], P(None, None, 'pairs', 'stripe')
Inputs may be any that keep to these rules, and one draw needn't show every extreme that they name: `pair_list`: rows g * 250 to (g + 1) * 250 - 1 form pair group g: their reference dates lie in g * 64 to (g + 1) * 64 - 1, each secondary date is 1 to 5 dates after its reference, and no pair repeats.
All inputs are finite; a program needn't handle non-finite values.
Results may differ from a plain program's by a relative error of at most 0.0029.
Values may be sent and summed in bfloat16 or wider, within the bound.
A program may use at most 64 MiB of HBM per device.

v0:
```python
from functools import partial

import jax
import jax.numpy as jnp
from jax import lax
from jax.sharding import PartitionSpec as P

MAXB = 5
LA = 4
LR = 16
MAXR = 16
FILTER_R = 3


damping = 0.5


def padded(value, sides, width):
    for axis, dim in sides:
        size, length = (lax.axis_size(axis), value.shape[dim])
        up = [(i, (i + 1) % size) for i in range(size - 1)]
        down = [(j, i) for i, j in up]
        last = lax.slice_in_dim(value, length - width, length, axis=dim)
        first = lax.slice_in_dim(value, 0, width, axis=dim)
        before = lax.ppermute(last, axis, up)
        after = lax.ppermute(first, axis, down)
        value = jnp.concatenate([before, value, after], axis=dim)
    return value


def from_behind(block, axis, distance):
    devices = range(lax.axis_size(axis))
    route = [(i - distance, i) for i in devices if i - distance in devices]
    return lax.ppermute(block, axis, route)


def azimuth_maps(az_shifts, az_lines):
    positions = jnp.arange(az_lines, dtype=jnp.int32)
    return (positions[None, None, :] == positions[None, :, None] + az_shifts[:, None, None]).astype(
        jnp.bfloat16
    )


def range_maps(rg_shifts, columns, margin):
    inputs = jnp.arange(columns + 2 * margin, dtype=jnp.int32)
    outputs = jnp.arange(columns, dtype=jnp.int32)
    return (
        inputs[None, :, None] == outputs[None, None, :] + margin + rg_shifts[:, None, None]
    ).astype(jnp.bfloat16)


def shift_lines(images, az_shifts):
    maps = azimuth_maps(az_shifts, images.shape[2])
    shifted = jnp.einsum("nik,nckj->ncij", maps, images, preferred_element_type=jnp.float32)
    return shifted.astype(jnp.bfloat16)


def resample_stripes(widened, az_shifts, rg_shifts):
    shifted = shift_lines(widened, az_shifts)
    columns = widened.shape[3] - 2 * MAXR
    result = jnp.einsum(
        "ncik,nkj->ncij",
        shifted,
        range_maps(rg_shifts, columns, MAXR),
        preferred_element_type=jnp.float32,
    )
    return result.astype(jnp.bfloat16)


def form_block(local_images, next_images, row_pool, col_pool, id_block):
    local_count = local_images.shape[0]
    next_count = next_images.shape[0]
    local_slots = jnp.arange(local_count, dtype=jnp.int32)
    next_slots = local_count + jnp.arange(next_count, dtype=jnp.int32)

    def select(date_ids):
        pick_local = (date_ids[:, None] == local_slots[None, :]).astype(jnp.bfloat16)
        pick_next = (date_ids[:, None] == next_slots[None, :]).astype(jnp.bfloat16)
        chosen = jnp.einsum(
            "pn,ncij->pcij", pick_local, local_images, preferred_element_type=jnp.float32
        )
        return chosen + jnp.einsum(
            "pm,mcij->pcij", pick_next, next_images, preferred_element_type=jnp.float32
        )

    ref_image = select(id_block[:, 0])
    sec_image = select(id_block[:, 1])
    real_part = ref_image[:, 0] * sec_image[:, 0] + ref_image[:, 1] * sec_image[:, 1]
    imag_part = ref_image[:, 1] * sec_image[:, 0] - ref_image[:, 0] * sec_image[:, 1]
    highest = lax.Precision.HIGHEST

    def pool(values):
        narrowed = jnp.einsum("pij,jv->piv", values, col_pool, precision=highest)
        return jnp.einsum("ui,piv->puv", row_pool, narrowed, precision=highest)

    looked = jnp.stack([pool(real_part), pool(imag_part)], axis=1)
    return (looked / (LA * LR)).astype(jnp.bfloat16)


def tap_value(offset_values):
    sigma = FILTER_R / 2.0
    spread = offset_values.astype(jnp.float32)
    return jnp.exp(-(spread * spread) / (2.0 * sigma * sigma))


def band_matrix(extent):
    outputs = jnp.arange(extent, dtype=jnp.int32)
    inputs = jnp.arange(extent + 2 * FILTER_R, dtype=jnp.int32)
    offsets = inputs[None, :] - outputs[:, None] - FILTER_R
    return jnp.where(jnp.abs(offsets) <= FILTER_R, tap_value(offsets), 0.0)


def edge_weights(start, extent, whole):
    positions = start + jnp.arange(extent, dtype=jnp.int32)
    reach = jnp.arange(-FILTER_R, FILTER_R + 1, dtype=jnp.int32)
    targets = positions[:, None] + reach[None, :]
    inside = (targets >= 0) & (targets < whole)
    return jnp.sum(jnp.where(inside, tap_value(reach)[None, :], 0.0), axis=1)


def local(slc_stack, az_offset, rg_offset, pair_list):
    stripe_count = lax.axis_size("stripe")
    group_count = lax.axis_size("pairs")
    date_total = az_offset.shape[0]
    block_dates = date_total // group_count
    group_index = lax.axis_index("pairs")
    local_dates = lax.all_to_all(slc_stack, "stripe", split_axis=3, concat_axis=0, tiled=True)
    widened = padded(local_dates, (("stripe", 3),), MAXR)
    leading = widened[:MAXB]
    following = from_behind(leading, "pairs", -1)
    local_ids_held = group_index * block_dates + jnp.arange(block_dates, dtype=jnp.int32)
    next_ids_held = jnp.minimum(
        (group_index + 1) * block_dates + jnp.arange(MAXB, dtype=jnp.int32), date_total - 1
    )
    local_images = resample_stripes(widened, az_offset[local_ids_held], rg_offset[local_ids_held])
    next_images = resample_stripes(following, az_offset[next_ids_held], rg_offset[next_ids_held])
    az_lines = local_images.shape[2]
    width_here = local_images.shape[3]
    line_ids = jnp.arange(az_lines, dtype=jnp.int32)
    row_pool = (
        jnp.arange(az_lines // LA, dtype=jnp.int32)[:, None] == line_ids[None, :] // LA
    ).astype(jnp.float32)
    sample_ids = jnp.arange(width_here, dtype=jnp.int32)
    col_pool = (
        sample_ids[:, None] // LR == jnp.arange(width_here // LR, dtype=jnp.int32)[None, :]
    ).astype(jnp.float32)
    pair_group = pair_list.shape[0] // group_count
    group_pairs = lax.dynamic_slice_in_dim(pair_list, group_index * pair_group, pair_group, 0)
    local_ids = group_pairs - group_index * block_dates
    block_size = 1
    for candidate in range(1, 11):
        if pair_group % candidate == 0:
            block_size = candidate
    id_blocks = local_ids.reshape(pair_group // block_size, block_size, 2)
    look_blocks = lax.map(
        partial(form_block, local_images, next_images, row_pool, col_pool), id_blocks
    )
    multilooked = look_blocks.reshape(pair_group, 2, look_blocks.shape[3], look_blocks.shape[4])
    date_ids = jnp.arange(date_total, dtype=jnp.int32)
    signed_design = (date_ids[:, None] == pair_list[None, :, 0]).astype(jnp.float32) - (
        date_ids[:, None] == pair_list[None, :, 1]
    ).astype(jnp.float32)
    transposed_design = signed_design.astype(jnp.bfloat16)
    normal = jnp.dot(transposed_design, transposed_design.T, preferred_element_type=jnp.float32)
    normal = normal + damping * jnp.eye(date_total, dtype=jnp.float32)
    pixel_block = lax.all_to_all(multilooked, "pairs", split_axis=2, concat_axis=0, tiled=True)
    block_shape = pixel_block.shape[1:]
    right_side = jnp.dot(
        transposed_design,
        pixel_block.reshape(pixel_block.shape[0], -1),
        preferred_element_type=jnp.float32,
    )
    factor = jnp.linalg.cholesky(normal)
    series = jax.scipy.linalg.cho_solve((factor, True), right_side).reshape(
        (date_total,) + tuple(block_shape)
    )
    padded_series = padded(series, (("pairs", 2), ("stripe", 3)), FILTER_R)
    rows_here = series.shape[2]
    cols_here = series.shape[3]
    highest = lax.Precision.HIGHEST
    smoothed = jnp.einsum("uw,dcwx->dcux", band_matrix(rows_here), padded_series, precision=highest)
    smoothed = jnp.einsum("dcux,vx->dcuv", smoothed, band_matrix(cols_here), precision=highest)
    row_weight = edge_weights(group_index * rows_here, rows_here, rows_here * group_count)
    col_weight = edge_weights(
        lax.axis_index("stripe") * cols_here, cols_here, cols_here * stripe_count
    )
    screen = smoothed / (row_weight[:, None] * col_weight[None, :])
    return (screen, series - screen)


def solution(mesh):
    return jax.shard_map(
        local,
        mesh=mesh,
        in_specs=(P(("pairs", "stripe"), None, None, None), P(), P(), P()),
        out_specs=(P(None, None, "pairs", "stripe"), P(None, None, "pairs", "stripe")),
        check_vma=False,
    )
```

profile of v0, /device:TPU:15, one launch (start us, length us, event | category | flops | bytes accessed | tf_op | source)
XLA Modules:
  0.0 365.5 jit_solution(17412928181011621381)
XLA Ops:
  0.6 11.2 %copy.60 = bf16[2,2,128,4096]{2,1,0,3:T(2,128)(2,1)} copy(bf16[2,2,128,4096]{3,2,1,0:T(8,128)(2,1)} %param.6) | data formatting | bytes 8388608 | tf_op args[0]
  11.8 8.9 %all-to-all-start = ((bf16[2,2,128,4096]{2,1,0,3:T(2,128)(2,1)}), bf16[2,2,128,4096]{2,1,0,3:T(2,128)(2,1)}, u32[]{:S(2)}, u32[]{:S(2)}) async-start(bf16[2,2,128,4096]{2,1,0,3:T(2,128)(2,1)} %copy.60), calls=%async_computation | async-start | bytes 8388608 | tf_op jit(solution)/shard_map/all_to_all | solution.py:127
  24.6 11.7 %cholesky.49 = f32[128,128]{1,0:T(8,128)S(1)} custom-call(f32[128,128]{1,0:T(8,128)S(1)} %cholesky.115), custom_call_target="Cholesky" | custom-call | tf_op jit(solution)/shard_map/jit(cholesky)/cholesky | solution.py:173
  36.4 9.8 %custom-call.18 = f32[1,128,128]{1,2,0:T(8,128)S(1)} custom-call(f32[1,128,128]{2,1,0:T(8,128)S(1)} %get-tuple-element.168), custom_call_target="InvertDiagBlocksLowerTriangular" | custom-call | tf_op jit(solution)/shard_map/jit(cholesky)/cholesky | solution.py:173
  46.7 11.7 %cholesky.103 = f32[128,128]{1,0:T(8,128)S(1)} custom-call(f32[128,128]{1,0:T(8,128)S(1)} %convolution_subtract_fusion.2), custom_call_target="Cholesky" | custom-call | tf_op jit(solution)/shard_map/jit(cholesky)/cholesky | solution.py:173
  60.4 3.7 %while.13 = (s32[]{:T(128)}, f32[256,256]{1,0:T(8,128)S(1)}, s32[2,2]{1,0:T(2,128)S(1)}, f32[2,128,128]{2,1,0:T(8,128)S(1)}, s32[]{:T(128)}) while((s32[]{:T(128)}, f32[256,256]{1,0:T(8,128)S(1)}, s32[2,2]{1,0:T(2,128)S(1)}, f32[2,128,128]{2,1,0:T(8,128)S(1)}, s32[]{:T(128)}) %tuple.70), condition=%wide.while_cond, body=%wide.while_body.sunk | while | flops 2 | bytes 131189 | solution.py:174
  64.1 19.9 %custom-call.19 = f32[2,128,128]{1,2,0:T(8,128)S(1)} custom-call(f32[2,128,128]{2,1,0:T(8,128)S(1)} %get-tuple-element.53), custom_call_target="InvertDiagBlocksLowerTriangular" | custom-call | tf_op jit(solution)/shard_map/jit(_cho_solve)/triangular_solve | solution.py:174
  84.0 4.7 %copy.61 = bf16[2,2,128,4096]{2,3,1,0:T(8,128)(2,1)} copy(bf16[2,2,128,4096]{2,1,0,3:T(2,128)(2,1)} %all-to-all-done) | data formatting | bytes 8388608 | tf_op jit(solution)/shard_map/all_to_all | solution.py:127
  88.8 6.5 %copy.62 = bf16[32,2,2,128,128]{4,3,2,1,0:T(8,128)(2,1)} copy(bf16[32,2,2,128,128]{3,4,0,2,1:T(8,128)(2,1)} %bitcast.201) | data formatting | bytes 8388608 | tf_op jit(solution)/shard_map/all_to_all | solution.py:127
  95.2 6.4 %copy.63 = bf16[64,2,128,128]{2,3,1,0:T(8,128)(2,1)} copy(bf16[64,2,128,128]{3,2,1,0:T(8,128)(2,1)} %bitcast.202) | data formatting | bytes 8388608 | tf_op jit(solution)/shard_map/all_to_all | solution.py:127
  103.0 3.1 collective-permute-start
  108.5 8.6 %collective-permute-done = bf16[64,2,128,16]{2,3,1,0:T(8,128)(2,1)S(1)} collective-permute-done((bf16[64,2,128,16]{2,3,1,0:T(8,128)(2,1)S(1)}, bf16[64,2,128,16]{2,3,1,0:T(8,128)(2,1)S(1)}, u32[]{:S(2)}, u32[]{:S(2)}) %collective-permute-start) | collective-permute-done | bytes 524320 | tf_op jit(solution)/shard_map/ppermute | solution.py:25
  117.1 5.8 %collective-permute-done.1 = bf16[64,2,128,16]{2,3,1,0:T(8,128)(2,1)S(1)} collective-permute-done((bf16[64,2,128,16]{2,3,1,0:T(8,128)(2,1)S(1)}, bf16[64,2,128,16]{2,3,1,0:T(8,128)(2,1)S(1)}, u32[]{:S(2)}, u32[]{:S(2)}) %collective-permute-start.1) | collective-permute-done | bytes 524320 | tf_op jit(solution)/shard_map/ppermute | solution.py:26
  123.9 4.3 %collective-permute-start.2 = (bf16[5,2,128,160]{2,3,1,0:T(8,128)(2,1)S(1)}, bf16[5,2,128,160]{2,3,1,0:T(8,128)(2,1)S(1)}, u32[]{:S(2)}, u32[]{:S(2)}) collective-permute-start(bf16[5,2,128,160]{2,3,1,0:T(8,128)(2,1)S(1)} %pad_maximum_fusion), channel_id=1, source_target_pairs={{32,0},{64,32},{96,64},{33,1},{65,33},{97,65},{34,2},{66,34},{98,6... | collective-permute-start | bytes 1228808 | tf_op jit(solution)/shard_map/ppermute | solution.py:34
  128.3 7.6 %fusion.58 = bf16[64,2,128,128]{3,2,1,0:T(8,128)(2,1)} fusion(bf16[64,2,128,16]{2,3,1,0:T(8,128)(2,1)S(1)} %collective-permute-done.1, bf16[64,2,128,128]{2,3,1,0:T(8,128)(2,1)} %copy.63, bf16[64,2,128,16]{2,3,1,0:T(8,128)(2,1)S(1)} %collective-permute-done, s32[64,128]{1,0:T(8,128)S(1)} %get-tuple-element.178, s32[64,128]{1,0:T(8,128)S(1)} %get-tuple-element.177), kind=kOutput, calls=%fused_computation.68 | convolution fusion | flops 1364983808 | bytes 9502720 | tf_op jit(solution)/shard_map/ncik,nkj->ncij/dot_general | solution.py:61
  135.8 6.9 %copy.67 = bf16[64,2,128,128]{3,0,2,1:T(8,128)(2,1)} copy(bf16[64,2,128,128]{3,2,1,0:T(8,128)(2,1)} %fusion.58) | data formatting | bytes 8388608
  143.6 185.5 %while.14 = (s32[]{:T(128)}, bf16[25,10,2,32,8]{3,4,2,1,0:T(8,128)(2,1)S(1)}, s32[25,10,2]{1,0,2:T(8,128)S(1)}, bf16[64,2,128,128]{3,0,2,1:T(8,128)(2,1)}, bf16[...) while((s32[]{:T(128)}, ...), condition=%wide.region_5.6_spmd.clone.clone, body=%wide.region_4.5_spmd.clone.clone.sunk | while | flops 131436904 | bytes 39238300 | solution.py:155
  158.6 3.1 fusion.193
  166.0 3.1 fusion.193
  180.8 3.1 fusion.193
  188.2 3.1 fusion.193
  203.1 3.1 fusion.193
  225.3 3.1 fusion.193
  247.6 3.1 fusion.193
  262.4 3.1 fusion.193
  284.7 3.1 fusion.193
  306.9 3.1 fusion.193
  330.9 3.7 %all-to-all-start.1 = ((bf16[250,2,32,8]{0,3,1,2:T(8,128)(2,1)}), bf16[250,2,32,8]{0,3,1,2:T(8,128)(2,1)S(1)}, u32[]{:S(2)}, u32[]{:S(2)}) async-start(bf16[250,2,32,8]{0,3,1,2:T(8,128)(2,1)} %copy.70), calls=%async_computation.1 | async-start | bytes 524288 | tf_op jit(solution)/shard_map/all_to_all | solution.py:166
  334.6 6.7 %all-to-all-done.1 = bf16[250,2,32,8]{0,3,1,2:T(8,128)(2,1)S(1)} async-done(((bf16[250,2,32,8]{0,3,1,2:T(8,128)(2,1)}), bf16[250,2,32,8]{0,3,1,2:T(8,128)(2,1)S(1)}, u32[]{:S(2)}, u32[]{:S(2)}) %all-to-all-start.1) | async-done | bytes 256032 | tf_op jit(solution)/shard_map/all_to_all | solution.py:166
  348.7 4.9 %collective-permute-done.4 = f32[256,2,3,8]{0,2,3,1:T(4,128)S(1)} collective-permute-done((f32[256,2,3,8]{0,2,3,1:T(4,128)S(1)}, f32[256,2,3,8]{0,2,3,1:T(4,128)S(1)}, u32[]{:S(2)}, u32[]{:S(2)}) %collective-permute-start.4) | collective-permute-done | bytes 49184 | tf_op jit(solution)/shard_map/ppermute | solution.py:26
  355.6 3.4 collective-permute-start.6
  359.0 4.9 %collective-permute-done.6 = f32[256,2,14,3]{0,2,3,1:T(8,128)S(1)} collective-permute-done((f32[256,2,14,3]{0,2,3,1:T(8,128)S(1)}, f32[256,2,14,3]{0,2,3,1:T(8,128)S(1)}, u32[]{:S(2)}, u32[]{:S(2)}) %collective-permute-start.6) | collective-permute-done | bytes 86048 | tf_op jit(solution)/shard_map/ppermute | solution.py:26
  (441 shorter events, 179.6 us)
Async XLA Ops:
  0.6 20.1 %copy-start = (s32[256]{0:T(256)S(1)}, s32[256]{0:T(256)}, u32[]{:S(2)}) copy-start(s32[256]{0:T(256)} %param.8) | copy-start | bytes 3076
  11.8 9.8 %copy-start.1 = (s32[256]{0:T(256)S(1)}, s32[256]{0:T(256)}, u32[]{:S(2)}) copy-start(s32[256]{0:T(256)} %param.7) | copy-start | bytes 3076
  11.8 11.9 %copy-start.3 = (s32[1000,2]{0,1:T(2,128)S(1)}, s32[1000,2]{0,1:T(2,128)}, u32[]{:S(2)}) copy-start(s32[1000,2]{0,1:T(2,128)} %param.9) | copy-start | bytes 24004
  11.8 72.2 %all-to-all-start = ((bf16[2,2,128,4096]{2,1,0,3:T(2,128)(2,1)}), bf16[2,2,128,4096]{2,1,0,3:T(2,128)(2,1)}, u32[]{:S(2)}, u32[]{:S(2)}) async-start(bf16[2,2,128,4096]{2,1,0,3:T(2,128)(2,1)} %copy.60), calls=%async_computation | async-start | bytes 8388608 | tf_op jit(solution)/shard_map/all_to_all | solution.py:127
  103.0 14.1 %collective-permute-start = (bf16[64,2,128,16]{2,3,1,0:T(8,128)(2,1)S(1)}, bf16[64,2,128,16]{2,3,1,0:T(8,128)(2,1)S(1)}, u32[]{:S(2)}, u32[]{:S(2)}) collective-permute-start(bf16[64,2,128,16]{2,3,1,0:T(8,128)(2,1)S(1)} %get-tuple-element.159), channel_id=1, source_target_pairs={{0,1},{1,2},{2,3},{3,4},{4,5},{5,6},{6,7},{7,8},{8,9},{9,10},{10,1... | collective-permute-start | bytes 1572872 | tf_op jit(solution)/shard_map/ppermute | solution.py:25
  106.1 16.8 %collective-permute-start.1 = (bf16[64,2,128,16]{2,3,1,0:T(8,128)(2,1)S(1)}, bf16[64,2,128,16]{2,3,1,0:T(8,128)(2,1)S(1)}, u32[]{:S(2)}, u32[]{:S(2)}) collective-permute-start(bf16[64,2,128,16]{2,3,1,0:T(8,128)(2,1)S(1)} %get-tuple-element.160), channel_id=1, source_target_pairs={{1,0},{2,1},{3,2},{4,3},{5,4},{6,5},{7,6},{8,7},{9,8},{10,9},{11,1... | collective-permute-start | bytes 1572872 | tf_op jit(solution)/shard_map/ppermute | solution.py:26
  123.9 18.8 %collective-permute-start.2 = (bf16[5,2,128,160]{2,3,1,0:T(8,128)(2,1)S(1)}, bf16[5,2,128,160]{2,3,1,0:T(8,128)(2,1)S(1)}, u32[]{:S(2)}, u32[]{:S(2)}) collective-permute-start(bf16[5,2,128,160]{2,3,1,0:T(8,128)(2,1)S(1)} %pad_maximum_fusion), channel_id=1, source_target_pairs={{32,0},{64,32},{96,64},{33,1},{65,33},{97,65},{34,2},{66,34},{98,6... | collective-permute-start | bytes 1228808 | tf_op jit(solution)/shard_map/ppermute | solution.py:34
  143.7 3.7 %copy-start.2 = (bf16[64,2,128,128]{3,0,2,1:T(8,128)(2,1)S(1)}, bf16[64,2,128,128]{3,0,2,1:T(8,128)(2,1)}, u32[]{:S(2)}) copy-start(bf16[64,2,128,128]{3,0,2,1:T(8,128)(2,1)} %get-tuple-element.284) | copy-start | bytes 12582916 | tf_op jit(solution)/shard_map/while
  151.1 3.7 %copy-start.2 = (bf16[64,2,128,128]{3,0,2,1:T(8,128)(2,1)S(1)}, bf16[64,2,128,128]{3,0,2,1:T(8,128)(2,1)}, u32[]{:S(2)}) copy-start(bf16[64,2,128,128]{3,0,2,1:T(8,128)(2,1)} %get-tuple-element.284) | copy-start | bytes 12582916 | tf_op jit(solution)/shard_map/while
  166.0 3.7 %copy-start.2 = (bf16[64,2,128,128]{3,0,2,1:T(8,128)(2,1)S(1)}, bf16[64,2,128,128]{3,0,2,1:T(8,128)(2,1)}, u32[]{:S(2)}) copy-start(bf16[64,2,128,128]{3,0,2,1:T(8,128)(2,1)} %get-tuple-element.284) | copy-start | bytes 12582916 | tf_op jit(solution)/shard_map/while
  173.4 3.7 %copy-start.2 = (bf16[64,2,128,128]{3,0,2,1:T(8,128)(2,1)S(1)}, bf16[64,2,128,128]{3,0,2,1:T(8,128)(2,1)}, u32[]{:S(2)}) copy-start(bf16[64,2,128,128]{3,0,2,1:T(8,128)(2,1)} %get-tuple-element.284) | copy-start | bytes 12582916 | tf_op jit(solution)/shard_map/while
  180.8 3.7 %copy-start.2 = (bf16[64,2,128,128]{3,0,2,1:T(8,128)(2,1)S(1)}, bf16[64,2,128,128]{3,0,2,1:T(8,128)(2,1)}, u32[]{:S(2)}) copy-start(bf16[64,2,128,128]{3,0,2,1:T(8,128)(2,1)} %get-tuple-element.284) | copy-start | bytes 12582916 | tf_op jit(solution)/shard_map/while
  188.2 3.7 %copy-start.2 = (bf16[64,2,128,128]{3,0,2,1:T(8,128)(2,1)S(1)}, bf16[64,2,128,128]{3,0,2,1:T(8,128)(2,1)}, u32[]{:S(2)}) copy-start(bf16[64,2,128,128]{3,0,2,1:T(8,128)(2,1)} %get-tuple-element.284) | copy-start | bytes 12582916 | tf_op jit(solution)/shard_map/while
  195.6 3.7 %copy-start.2 = (bf16[64,2,128,128]{3,0,2,1:T(8,128)(2,1)S(1)}, bf16[64,2,128,128]{3,0,2,1:T(8,128)(2,1)}, u32[]{:S(2)}) copy-start(bf16[64,2,128,128]{3,0,2,1:T(8,128)(2,1)} %get-tuple-element.284) | copy-start | bytes 12582916 | tf_op jit(solution)/shard_map/while
  203.1 3.7 %copy-start.2 = (bf16[64,2,128,128]{3,0,2,1:T(8,128)(2,1)S(1)}, bf16[64,2,128,128]{3,0,2,1:T(8,128)(2,1)}, u32[]{:S(2)}) copy-start(bf16[64,2,128,128]{3,0,2,1:T(8,128)(2,1)} %get-tuple-element.284) | copy-start | bytes 12582916 | tf_op jit(solution)/shard_map/while
  210.5 3.7 %copy-start.2 = (bf16[64,2,128,128]{3,0,2,1:T(8,128)(2,1)S(1)}, bf16[64,2,128,128]{3,0,2,1:T(8,128)(2,1)}, u32[]{:S(2)}) copy-start(bf16[64,2,128,128]{3,0,2,1:T(8,128)(2,1)} %get-tuple-element.284) | copy-start | bytes 12582916 | tf_op jit(solution)/shard_map/while
  217.9 3.7 %copy-start.2 = (bf16[64,2,128,128]{3,0,2,1:T(8,128)(2,1)S(1)}, bf16[64,2,128,128]{3,0,2,1:T(8,128)(2,1)}, u32[]{:S(2)}) copy-start(bf16[64,2,128,128]{3,0,2,1:T(8,128)(2,1)} %get-tuple-element.284) | copy-start | bytes 12582916 | tf_op jit(solution)/shard_map/while
  225.3 3.7 %copy-start.2 = (bf16[64,2,128,128]{3,0,2,1:T(8,128)(2,1)S(1)}, bf16[64,2,128,128]{3,0,2,1:T(8,128)(2,1)}, u32[]{:S(2)}) copy-start(bf16[64,2,128,128]{3,0,2,1:T(8,128)(2,1)} %get-tuple-element.284) | copy-start | bytes 12582916 | tf_op jit(solution)/shard_map/while
  232.7 3.7 %copy-start.2 = (bf16[64,2,128,128]{3,0,2,1:T(8,128)(2,1)S(1)}, bf16[64,2,128,128]{3,0,2,1:T(8,128)(2,1)}, u32[]{:S(2)}) copy-start(bf16[64,2,128,128]{3,0,2,1:T(8,128)(2,1)} %get-tuple-element.284) | copy-start | bytes 12582916 | tf_op jit(solution)/shard_map/while
  240.2 3.7 %copy-start.2 = (bf16[64,2,128,128]{3,0,2,1:T(8,128)(2,1)S(1)}, bf16[64,2,128,128]{3,0,2,1:T(8,128)(2,1)}, u32[]{:S(2)}) copy-start(bf16[64,2,128,128]{3,0,2,1:T(8,128)(2,1)} %get-tuple-element.284) | copy-start | bytes 12582916 | tf_op jit(solution)/shard_map/while
  247.6 3.7 %copy-start.2 = (bf16[64,2,128,128]{3,0,2,1:T(8,128)(2,1)S(1)}, bf16[64,2,128,128]{3,0,2,1:T(8,128)(2,1)}, u32[]{:S(2)}) copy-start(bf16[64,2,128,128]{3,0,2,1:T(8,128)(2,1)} %get-tuple-element.284) | copy-start | bytes 12582916 | tf_op jit(solution)/shard_map/while
  255.0 3.7 %copy-start.2 = (bf16[64,2,128,128]{3,0,2,1:T(8,128)(2,1)S(1)}, bf16[64,2,128,128]{3,0,2,1:T(8,128)(2,1)}, u32[]{:S(2)}) copy-start(bf16[64,2,128,128]{3,0,2,1:T(8,128)(2,1)} %get-tuple-element.284) | copy-start | bytes 12582916 | tf_op jit(solution)/shard_map/while
  262.4 3.7 %copy-start.2 = (bf16[64,2,128,128]{3,0,2,1:T(8,128)(2,1)S(1)}, bf16[64,2,128,128]{3,0,2,1:T(8,128)(2,1)}, u32[]{:S(2)}) copy-start(bf16[64,2,128,128]{3,0,2,1:T(8,128)(2,1)} %get-tuple-element.284) | copy-start | bytes 12582916 | tf_op jit(solution)/shard_map/while
  284.7 3.7 %copy-start.2 = (bf16[64,2,128,128]{3,0,2,1:T(8,128)(2,1)S(1)}, bf16[64,2,128,128]{3,0,2,1:T(8,128)(2,1)}, u32[]{:S(2)}) copy-start(bf16[64,2,128,128]{3,0,2,1:T(8,128)(2,1)} %get-tuple-element.284) | copy-start | bytes 12582916 | tf_op jit(solution)/shard_map/while
  299.5 3.7 %copy-start.2 = (bf16[64,2,128,128]{3,0,2,1:T(8,128)(2,1)S(1)}, bf16[64,2,128,128]{3,0,2,1:T(8,128)(2,1)}, u32[]{:S(2)}) copy-start(bf16[64,2,128,128]{3,0,2,1:T(8,128)(2,1)} %get-tuple-element.284) | copy-start | bytes 12582916 | tf_op jit(solution)/shard_map/while
  306.9 3.7 %copy-start.2 = (bf16[64,2,128,128]{3,0,2,1:T(8,128)(2,1)S(1)}, bf16[64,2,128,128]{3,0,2,1:T(8,128)(2,1)}, u32[]{:S(2)}) copy-start(bf16[64,2,128,128]{3,0,2,1:T(8,128)(2,1)} %get-tuple-element.284) | copy-start | bytes 12582916 | tf_op jit(solution)/shard_map/while
  321.8 3.7 %copy-start.2 = (bf16[64,2,128,128]{3,0,2,1:T(8,128)(2,1)S(1)}, bf16[64,2,128,128]{3,0,2,1:T(8,128)(2,1)}, u32[]{:S(2)}) copy-start(bf16[64,2,128,128]{3,0,2,1:T(8,128)(2,1)} %get-tuple-element.284) | copy-start | bytes 12582916 | tf_op jit(solution)/shard_map/while
  330.9 10.4 %all-to-all-start.1 = ((bf16[250,2,32,8]{0,3,1,2:T(8,128)(2,1)}), bf16[250,2,32,8]{0,3,1,2:T(8,128)(2,1)S(1)}, u32[]{:S(2)}, u32[]{:S(2)}) async-start(bf16[250,2,32,8]{0,3,1,2:T(8,128)(2,1)} %copy.70), calls=%async_computation.1 | async-start | bytes 524288 | tf_op jit(solution)/shard_map/all_to_all | solution.py:166
  343.8 4.9 %collective-permute-start.3 = (f32[256,2,3,8]{0,2,3,1:T(4,128)S(1)}, f32[256,2,3,8]{0,2,3,1:T(4,128)S(1)}, u32[]{:S(2)}, u32[]{:S(2)}) collective-permute-start(f32[256,2,3,8]{0,2,3,1:T(4,128)S(1)} %get-tuple-element.163), channel_id=1, source_target_pairs={{0,32},{32,64},{64,96},{1,33},{33,65},{65,97},{2,34},{34,66},{66,9... | collective-permute-start | bytes 147464 | tf_op jit(solution)/shard_map/ppermute | solution.py:25
  346.5 7.1 %collective-permute-start.4 = (f32[256,2,3,8]{0,2,3,1:T(4,128)S(1)}, f32[256,2,3,8]{0,2,3,1:T(4,128)S(1)}, u32[]{:S(2)}, u32[]{:S(2)}) collective-permute-start(f32[256,2,3,8]{0,2,3,1:T(4,128)S(1)} %get-tuple-element.164), channel_id=1, source_target_pairs={{32,0},{64,32},{96,64},{33,1},{65,33},{97,65},{34,2},{66,34},{98,6... | collective-permute-start | bytes 147464 | tf_op jit(solution)/shard_map/ppermute | solution.py:26
  353.7 5.4 %collective-permute-start.5 = (f32[256,2,14,3]{0,2,3,1:T(8,128)S(1)}, f32[256,2,14,3]{0,2,3,1:T(8,128)S(1)}, u32[]{:S(2)}, u32[]{:S(2)}) collective-permute-start(f32[256,2,14,3]{0,2,3,1:T(8,128)S(1)} %get-tuple-element.161), channel_id=1, source_target_pairs={{0,1},{1,2},{2,3},{3,4},{4,5},{5,6},{6,7},{7,8},{8,9},{9,10},{10,1... | collective-permute-start | bytes 258056 | tf_op jit(solution)/shard_map/ppermute | solution.py:25
  355.6 8.4 %collective-permute-start.6 = (f32[256,2,14,3]{0,2,3,1:T(8,128)S(1)}, f32[256,2,14,3]{0,2,3,1:T(8,128)S(1)}, u32[]{:S(2)}, u32[]{:S(2)}) collective-permute-start(f32[256,2,14,3]{0,2,3,1:T(8,128)S(1)} %get-tuple-element.162), channel_id=1, source_target_pairs={{1,0},{2,1},{3,2},{4,3},{5,4},{6,5},{7,6},{8,7},{9,8},{10,9},{11,1... | collective-permute-start | bytes 258056 | tf_op jit(solution)/shard_map/ppermute | solution.py:26
  (5 other events, 18.5 us)
where the time goes:
time: 367 us; the launch traced here: 366 us
  matrix products  187 us (51%)
  other arithmetic  63.1 us (17%)
  local copies, waits for them, and re-layouts  47.1 us (13%)
  starting transfers between devices  32.2 us (9%)
  waiting for transfers between devices  31 us (8%)
    dot_general x50, matrix products, select(): jnp.einsum('pn,ncij->pcij', pick_local, local_images, preferred_element_t...  94.4 us
    dot_general x50, matrix products, pool(): narrowed = jnp.einsum('pij,jv->piv', values, col_pool, precision=highest)  39.1 us
    another operation x6, other arithmetic, local(): factor = jnp.linalg.cholesky(normal)  34 us
    dot_general x50, matrix products, select(): jnp.einsum('pm,mcij->pcij', pick_next, next_images, preferred_element_typ...  30.7 us
    another operation x4, other arithmetic, local(): jax.scipy.linalg.cho_solve((factor, True), right_side)  19.9 us
    unnamed x9, local copies, waits for them, and re-layouts  18.3 us
    all_to_all x3, local copies, waits for them, and re-layouts, local(): lax.all_to_all(slc_stack, 'stripe', split_axis=3, concat_axis=0, tiled=True)  17.6 us
    ppermute x3, waiting for transfers between devices, padded(): after = lax.ppermute(first, axis, down)  15.7 us
  transfers between devices with their start and end apart: 9, of which 5 were waited for; matrix products, arithmetic and copies ran while one was open for 21% of the time, Pallas kernels for 0%

commit v1 on v0

v1 whole, which is shorter than its diff:
```python
import math

import jax
import jax.numpy as jnp
from jax import lax
from jax.experimental import pallas as pl
from jax.experimental.pallas import tpu as pltpu
from jax.sharding import PartitionSpec as P

MESH = pl.DeviceIdType.MESH
HIGHEST = lax.Precision.HIGHEST
F32 = jnp.float32
BF16 = jnp.bfloat16

GROUPS = 4
STRIPES = 32
DATES = 256
BLOCK = 64
GAPS = 5
COMBOS = BLOCK * GAPS
AHEAD = 3
LINES = 128
CHUNK = LINES // GROUPS
WIDTH = 128
RANGE = STRIPES * WIDTH
TILE = 128
MROWS = 8
ROWS = 72
LIST = 1024
RADIUS = 3
DAMPING = 0.5
NEWTON = 9
START = 2.0 / 21.0
SPREAD = 2.0 * (RADIUS / 2.0) ** 2


def iota(shape, dim):
    return lax.broadcasted_iota(jnp.int32, shape, dim)


def dot(a, b, precision=None):
    return lax.dot_general(
        a, b, (((1,), (0,)), ((), ())), precision=precision, preferred_element_type=F32
    )


def dot_lanes(a, b):
    return lax.dot_general(a, b, (((1,), (1,)), ((), ())), preferred_element_type=F32)


def offset_of(k):
    n = lax.rem(k + 1, 4)
    dx = n + n // 2 - 2 * (n // 3)
    dy = 1 - lax.rem(k, 8) // 4
    dz = lax.rem(dx + k // 8, 4)
    return dz, dy, dx


SELF = 7


def edge_weight(position, whole):
    total = jnp.zeros(position.shape, F32)
    for k in range(-RADIUS, RADIUS + 1):
        inside = (position + k >= 0) & (position + k < whole)
        total = total + jnp.where(inside, F32(math.exp(-k * k / SPREAD)), F32(0))
    return total


def tap(offset):
    spread = offset.astype(F32)
    return jnp.where(jnp.abs(offset) <= RADIUS, jnp.exp(-(spread * spread) / SPREAD), 0.0)


def kernel(
    slc, az, rg, pairs_in, screen_out, motion_out,
    image, send, recv, acc, smap, rmap, plist, normal, inverse, design, weights,
    right, blocks, total, image_sem, send_sem, recv_sem, lend_sem, borrow_sem, part_send, part_recv,
):
    p = lax.axis_index("pairs")
    s = lax.axis_index("stripe")
    sz, sy, sx = s // 8, lax.rem(s // 4, 2), lax.rem(s, 4)

    loads = []
    for j in range(2):
        for c in range(2):
            load = pltpu.make_async_copy(
                slc.at[j, c],
                image.at[j, pl.ds(c * LINES, LINES), pl.ds(WIDTH, RANGE)],
                image_sem.at[2 * j + c],
            )
            load.start()
            loads.append(load)

    def peer(k):
        dz, dy, dx = offset_of(k)
        return lax.rem(sz + dz, 4) * 8 + lax.rem(sy + dy, 2) * 4 + lax.rem(sx + dx, 4)

    barrier = pltpu.get_barrier_semaphore()

    def greet(i, carry):
        pl.semaphore_signal(
            barrier, inc=1, device_id=(p, lax.rem(s + i, STRIPES)), device_id_type=MESH
        )
        return carry

    lax.fori_loop(1, STRIPES, greet, 0)
    for dp in range(1, GROUPS):
        for ds in (-1, 0, 1):
            pl.semaphore_signal(
                barrier,
                inc=1,
                device_id=(lax.rem(p + dp, GROUPS), lax.rem(s + ds + STRIPES, STRIPES)),
                device_id_type=MESH,
            )

    for j in range(2):
        date = p * BLOCK + s * 2 + j
        row = iota((LINES, LINES), 0)
        line = (row & ~31) + ((row & 7) << 2) + ((row >> 3) & 3)
        smap[j] = (iota((LINES, LINES), 1) == line + az[date]).astype(BF16)
        rmap[j] = (
            iota((3 * WIDTH, WIDTH), 0) == iota((3 * WIDTH, WIDTH), 1) + WIDTH + rg[date]
        ).astype(BF16)
        edge = jnp.zeros((2 * LINES, WIDTH), BF16)
        image[j, :, pl.ds(0, WIDTH)] = edge
        image[j, :, pl.ds(WIDTH + RANGE, WIDTH)] = edge
    for load in loads:
        load.wait()
    pl.semaphore_wait(barrier, STRIPES - 1 + 3 * (GROUPS - 1))

    def stripe_copy(c, k):
        target = peer(k)
        return pltpu.make_async_remote_copy(
            src_ref=send.at[c, target],
            dst_ref=recv.at[c, pl.ds(s * TILE, TILE)],
            send_sem=send_sem.at[c, k],
            recv_sem=recv_sem.at[c, k],
            device_id=(p, target),
            device_id_type=MESH,
        )

    def resample(k, carry):
        target = peer(k)
        start = pl.multiple_of(target * WIDTH, WIDTH)
        for j in range(2):
            moved = dot(image[j, :, pl.ds(start, 3 * WIDTH)], rmap[j]).astype(BF16)
            both = jnp.concatenate([moved[:LINES], moved[LINES:]], axis=1)
            shifted = dot(smap[j], both).astype(BF16)
            for c in range(GROUPS):
                for comp in range(2):
                    send[c, target, pl.ds(j * 64 + comp * CHUNK, CHUNK), :] = shifted[
                        c * CHUNK : (c + 1) * CHUNK, comp * WIDTH : (comp + 1) * WIDTH
                    ]

        @pl.when(k != SELF)
        def _():
            stripe_copy(0, k).start()

        return carry

    lax.fori_loop(0, STRIPES, resample, 0)

    for c in range(1, GROUPS):

        def launch(k, carry, c=c):
            @pl.when(k != SELF)
            def _():
                stripe_copy(c, k).start()

            return carry

        lax.fori_loop(0, STRIPES, launch, 0)

    for c in range(GROUPS):
        recv[c, pl.ds(s * TILE, TILE), :] = send[c, s]

    plist[...] = jnp.full((8, LIST), -100000, jnp.int32)
    plist[0:2, 0:1000] = pairs_in[...]
    refs, secs = plist[0:1, :], plist[1:2, :]
    ids = iota((DATES, LIST), 0)
    signed = ((ids == refs).astype(F32) - (ids == secs).astype(F32)).astype(BF16)
    eye = (iota((DATES, DATES), 0) == iota((DATES, DATES), 1)).astype(F32)
    normal[...] = dot_lanes(signed, signed) + F32(DAMPING) * eye
    inverse[...] = F32(START) * eye

    def newton(_, carry):
        held = inverse[...]
        inverse[...] = 2.0 * held - dot(held, dot(normal[...], held, HIGHEST), HIGHEST)
        return carry

    lax.fori_loop(0, NEWTON, newton, 0)

    local = refs - p * BLOCK
    inside = (local >= 0) & (local < BLOCK)
    code = jnp.where(inside, (secs - refs - 1) * BLOCK + local, -1)
    found = (iota((COMBOS, LIST), 0) == code).astype(F32).astype(BF16)
    present = dot_lanes(jnp.ones((8, LIST), BF16), found)[0:1, :]
    combo = iota((ROWS, COMBOS), 1)
    first = combo & (BLOCK - 1)
    second = first + (combo >> 6) + 1
    place = iota((ROWS, COMBOS), 0)
    plain = (place == first).astype(F32) - (place == second).astype(F32)
    design[...] = (plain * present).astype(BF16)

    held_in, held_out = iota((128, 128), 0), iota((128, 128), 1)
    same = (held_in >> 6) == (held_out >> 6)
    row_in, row_out = (held_in >> 3) & 7, (held_out >> 3) & 7
    col_in, col_out = held_in & 7, held_out & 7
    scale = edge_weight(row_out + p * MROWS, MROWS * GROUPS) * edge_weight(
        col_out + s * MROWS, MROWS * STRIPES
    )
    for ci in range(3):
        far = row_in + (p + ci - 1) * MROWS
        near = row_out + p * MROWS
        row_ok = same & (far >= 0) & (far < MROWS * GROUPS)
        row_tap = jnp.where(row_ok, tap(far - near), 0.0)
        for si in range(3):
            far = col_in + (s + si - 1) * MROWS
            near = col_out + s * MROWS
            col_ok = (far >= 0) & (far < MROWS * STRIPES)
            col_tap = jnp.where(col_ok, tap(far - near), 0.0)
            weights[3 * ci + si] = row_tap * col_tap / scale
    total[...] = jnp.zeros(total.shape, F32)

    def lend(c):
        return pltpu.make_async_remote_copy(
            src_ref=recv.at[c, pl.ds(0, AHEAD * TILE)],
            dst_ref=recv.at[c, pl.ds(STRIPES * TILE, AHEAD * TILE)],
            send_sem=lend_sem.at[c],
            recv_sem=borrow_sem.at[c],
            device_id=(lax.rem(p + GROUPS - 1, GROUPS), s),
            device_id_type=MESH,
        )

    def part(c, ci, ds):
        target = (c - ci + GROUPS) % GROUPS
        rel = lax.rem(p - target + GROUPS, GROUPS)
        slot = 3 * (ci + 1) + 1 - ds
        source = right.at[c]
        landing = blocks.at[slot, pl.ds(pl.multiple_of(rel * ROWS, 8), ROWS)]
        remote = pltpu.make_async_remote_copy(
            src_ref=source,
            dst_ref=landing,
            send_sem=part_send.at[c, slot],
            recv_sem=part_recv.at[rel, slot],
            device_id=(target, lax.rem(s + ds + STRIPES, STRIPES)),
            device_id_type=MESH,
        )
        return target, slot, rel, remote

    def chunk(c, carry):
        def arrive(k, inner):
            @pl.when(k != SELF)
            def _():
                arriving = stripe_copy(c, k)
                arriving.wait_send()
                arriving.wait_recv()

            return inner

        lax.fori_loop(0, STRIPES, arrive, 0)
        lend(c).start()

        def products(d, inner):
            base = pl.multiple_of(d * 64, 64)

            def held(offset):
                lines = recv[c, pl.ds(base + offset, CHUNK), :].astype(F32)
                return lines.reshape(4, MROWS, WIDTH)

            a, b = held(0), held(CHUNK)
            for gap in range(1, GAPS + 1):
                x, y = held(64 * gap), held(64 * gap + CHUNK)
                real = jnp.sum(a * x + b * y, axis=0)
                imag = jnp.sum(b * x - a * y, axis=0)
                row = pl.multiple_of(((gap - 1) * BLOCK + d) * 16, 16)
                acc[pl.ds(row, MROWS), :] = real
                acc[pl.ds(row + MROWS, MROWS), :] = imag
            return inner

        lax.fori_loop(0, BLOCK - GAPS, products, 0)
        lend(c).wait_recv()
        lax.fori_loop(BLOCK - GAPS, BLOCK, products, 0)

        looked = jnp.zeros((COMBOS, 128), F32)
        lane = iota((2 * WIDTH, 128), 0) & (WIDTH - 1)
        column = iota((2 * WIDTH, 128), 1)
        for q in range(16):
            summed = acc[pl.ds(q, COMBOS, stride=16), :]
            high = summed.astype(BF16)
            low = (summed - high.astype(F32)).astype(BF16)
            pool = jnp.where(column == q * MROWS + (lane >> 4), 1.0 / 64.0, 0.0).astype(BF16)
            looked = looked + dot(jnp.concatenate([high, low], axis=1), pool)
        right[c] = dot(design[...], looked.astype(BF16))
        return carry

    for c in range(GROUPS):
        chunk(c, 0)
        for ci in (-1, 0, 1):
            for ds in (-1, 0, 1):
                target, slot, rel, remote = part(c, ci, ds)
                if ds == 0:

                    @pl.when(target != p)
                    def _():
                        remote.start()

                    @pl.when(target == p)
                    def _():
                        blocks[slot, 0:ROWS, :] = right[c]
                else:
                    remote.start()
        lend(c).wait_send()

    for c in range(GROUPS):
        for ci in (-1, 0, 1):
            for ds in (-1, 0, 1):
                target, slot, rel, remote = part(c, ci, ds)
                if ds == 0:

                    @pl.when(target != p)
                    def _():
                        remote.wait_send()
                else:
                    remote.wait_send()
    for rel in range(GROUPS):
        for slot in range(9):
            if rel == 0 and slot % 3 == 1:
                continue
            pltpu.make_async_remote_copy(
                src_ref=right.at[0],
                dst_ref=blocks.at[slot, pl.ds(rel * ROWS, ROWS)],
                send_sem=part_send.at[0, slot],
                recv_sem=part_recv.at[rel, slot],
                device_id=(lax.rem(p + 1, GROUPS), s),
                device_id_type=MESH,
            ).wait_recv()

    smooth = dot(blocks[0], weights[0], HIGHEST)
    for slot in range(1, 9):
        smooth = smooth + dot(blocks[slot], weights[slot], HIGHEST)
    centre = blocks[4]
    for rel in range(GROUPS):
        group = lax.rem(p + rel, GROUPS)
        rows = pl.ds(pl.multiple_of(group * BLOCK, BLOCK), ROWS)
        cut = slice(rel * ROWS, (rel + 1) * ROWS)
        total[rows, 0:128] = total[rows, 0:128] + centre[cut]
        total[rows, 128:256] = total[rows, 128:256] + smooth[cut]
    solved = dot(inverse[...], total[0:DATES, :], HIGHEST)
    screen = solved[:, 128:256]
    screen_out[...] = screen.T
    motion_out[...] = (solved[:, 0:128] - screen).T


def local(slc_stack, az_offset, rg_offset, pair_list):
    vmem = pl.BlockSpec(memory_space=pltpu.VMEM)
    smem = pl.BlockSpec(memory_space=pltpu.SMEM)
    dma = pltpu.SemaphoreType.DMA
    result = jax.ShapeDtypeStruct((2 * MROWS * MROWS, DATES), F32)
    screen, motion = pl.pallas_call(
        kernel,
        out_shape=(result, result),
        in_specs=[pl.BlockSpec(memory_space=pl.ANY), smem, smem, vmem],
        out_specs=(vmem, vmem),
        scratch_shapes=[
            pltpu.VMEM((2, 2 * LINES, RANGE + 2 * WIDTH), BF16),
            pltpu.VMEM((GROUPS, STRIPES, TILE, WIDTH), BF16),
            pltpu.VMEM((GROUPS, (STRIPES + AHEAD) * TILE, WIDTH), BF16),
            pltpu.VMEM((COMBOS * 16, WIDTH), F32),
            pltpu.VMEM((2, LINES, LINES), BF16),
            pltpu.VMEM((2, 3 * WIDTH, WIDTH), BF16),
            pltpu.VMEM((8, LIST), jnp.int32),
            pltpu.VMEM((DATES, DATES), F32),
            pltpu.VMEM((DATES, DATES), F32),
            pltpu.VMEM((ROWS, COMBOS), BF16),
            pltpu.VMEM((9, 128, 128), F32),
            pltpu.VMEM((GROUPS, ROWS, 128), F32),
            pltpu.VMEM((9, GROUPS * ROWS, 128), F32),
            pltpu.VMEM(((GROUPS - 1) * BLOCK + ROWS, 256), F32),
            dma((4,)),
            dma((GROUPS, STRIPES)),
            dma((GROUPS, STRIPES)),
            dma((GROUPS,)),
            dma((GROUPS,)),
            dma((GROUPS, 9)),
            dma((GROUPS, 9)),
        ],
        compiler_params=pltpu.CompilerParams(
            collective_id=0, has_side_effects=True, vmem_limit_bytes=48 << 20
        ),
    )(slc_stack, az_offset, rg_offset, pair_list.T)

    def placed(value):
        return value.reshape(2, MROWS, MROWS, DATES).transpose(3, 0, 1, 2)

    return placed(screen), placed(motion)


def solution(mesh):
    return jax.shard_map(
        local,
        mesh=mesh,
        in_specs=(P(("pairs", "stripe"), None, None, None), P(), P(), P()),
        out_specs=(P(None, None, "pairs", "stripe"), P(None, None, "pairs", "stripe")),
        check_vma=False,
    )
```

time: 367 us -> 108 us (0.29)
  the two profiles are of different devices: /device:TPU:15 before, /device:TPU:25 now
where the time goes in v1:
time: 108 us; the launch traced here: 107 us
  Pallas kernels  100 us (93%)
  local copies, waits for them, and re-layouts  5.55 us (5%)
    pallas_call x1, Pallas kernels, local(): pl.pallas_call(kernel, out_shape=(result, result), in_specs=[pl.BlockSpec...  100 us
    unnamed x10, local copies, waits for them, and re-layouts  5.55 us

profile of v1, /device:TPU:25, one launch (start us, length us, event | category | flops | bytes accessed | tf_op | source)
XLA Modules:
  0.0 106.5 jit_solution(8989014652677511089)
XLA Ops:
  0.6 0.0 copy-start
  0.6 2.2 %copy-done = bf16[2,2,128,4096]{3,2,1,0:T(8,128)(2,1)S(1)} copy-done((bf16[2,2,128,4096]{3,2,1,0:T(8,128)(2,1)S(1)}, bf16[2,2,128,4096]{3,2,1,0:T(8,128)(2,1)}, u32[]{:S(2)}) %copy-start) | copy-done | bytes 4194328
  2.8 0.0 copy-start.1
  2.8 0.7 copy-done.1
  3.5 0.0 copy-start.2
  3.5 0.7 copy-done.2
  4.2 0.0 copy-start.3
  4.2 0.7 copy-done.3
  4.9 100.3 %shard_map.59 = (f32[128,256]{1,0:T(8,128)S(1)}, f32[128,256]{1,0:T(8,128)S(1)}) custom-call(bf16[2,2,128,4096]{3,2,1,0:T(8,128)(2,1)S(1)} %copy-done, s32[256]{0:T(256)S(1)} %copy-done.2, s32[256]{0:T(256)S(1)} %copy-done.3, s32[2,1000]{1,0:T(2,128)S(1)} %bitcast.9), custom_call_target="tpu_custom_call" | custom-call | tf_op jit(solution)/shard_map/pallas_call | solution.py:361
  105.2 0.7 copy.8
  105.9 0.7 copy.9
Async XLA Ops:
  0.6 2.2 %copy-start = (bf16[2,2,128,4096]{3,2,1,0:T(8,128)(2,1)S(1)}, bf16[2,2,128,4096]{3,2,1,0:T(8,128)(2,1)}, u32[]{:S(2)}) copy-start(bf16[2,2,128,4096]{3,2,1,0:T(8,128)(2,1)} %slc.1) | copy-start | bytes 12582916
  2.8 0.7 copy-start.1
  3.5 0.7 copy-start.2
  4.2 0.7 copy-start.3

commit v2 on v1

--- a/solution.py
+++ b/solution.py
@@ -18,7 +18,7 @@
 BLOCK = 64
 GAPS = 5
 COMBOS = BLOCK * GAPS
-AHEAD = 3
+LENT = GAPS * 64
 LINES = 128
 CHUNK = LINES // GROUPS
 WIDTH = 128
@@ -30,6 +30,7 @@
 RADIUS = 3
 DAMPING = 0.5
 NEWTON = 9
+EAGER = 2
 START = 2.0 / 21.0
 SPREAD = 2.0 * (RADIUS / 2.0) ** 2
 
@@ -73,14 +74,18 @@
 
 
 def kernel(
-    slc, az, rg, pairs_in, screen_out, motion_out,
-    image, send, recv, acc, smap, rmap, plist, normal, inverse, design, weights,
-    right, blocks, total, image_sem, send_sem, recv_sem, lend_sem, borrow_sem, part_send, part_recv,
+    slc, az_in, rg_in, pairs_in, screen_out, motion_out,
+    az, rg, listed, image, send, recv, acc, smap, rmap, plist, normal, inverse, design, row_taps, col_taps, scale,
+    right, blocks, total, small_sem, image_sem, send_sem, recv_sem, lend_sem, borrow_sem, part_send, part_recv,
 ):
     p = lax.axis_index("pairs")
     s = lax.axis_index("stripe")
     sz, sy, sx = s // 8, lax.rem(s // 4, 2), lax.rem(s, 4)
 
+    small = []
+    for n, (source, held) in enumerate(((az_in, az), (rg_in, rg), (pairs_in, listed))):
+        small.append(pltpu.make_async_copy(source, held, small_sem.at[n]))
+        small[n].start()
     loads = []
     for j in range(2):
         for c in range(2):
@@ -96,6 +101,13 @@
         dz, dy, dx = offset_of(k)
         return lax.rem(sz + dz, 4) * 8 + lax.rem(sy + dy, 2) * 4 + lax.rem(sx + dx, 4)
 
+    def turn_of(source):
+        dz = lax.rem(sz - source // 8 + 4, 4)
+        dy = lax.rem(sy - lax.rem(source // 4, 2) + 2, 2)
+        dx = lax.rem(sx - lax.rem(source, 4) + 4, 4)
+        n = dx + dx // 2 - 2 * (dx // 3)
+        return lax.rem(dz - dx + 4, 4) * 8 + (1 - dy) * 4 + lax.rem(n + 3, 4)
+
     barrier = pltpu.get_barrier_semaphore()
 
     def greet(i, carry):
@@ -114,6 +126,8 @@
                 device_id_type=MESH,
             )
 
+    for load in small:
+        load.wait()
     for j in range(2):
         date = p * BLOCK + s * 2 + j
         row = iota((LINES, LINES), 0)
@@ -155,13 +169,14 @@
 
         @pl.when(k != SELF)
         def _():
-            stripe_copy(0, k).start()
+            for c in range(EAGER):
+                stripe_copy(c, k).start()
 
         return carry
 
-    lax.fori_loop(0, STRIPES, resample, 0)
-
-    for c in range(1, GROUPS):
+    lax.fori_loop(0, STRIPES, resample, 0, unroll=2)
+
+    for c in range(EAGER, GROUPS):
 
         def launch(k, carry, c=c):
             @pl.when(k != SELF)
@@ -176,7 +191,7 @@
         recv[c, pl.ds(s * TILE, TILE), :] = send[c, s]
 
     plist[...] = jnp.full((8, LIST), -100000, jnp.int32)
-    plist[0:2, 0:1000] = pairs_in[...]
+    plist[0:2, 0:1000] = listed[...]
     refs, secs = plist[0:1, :], plist[1:2, :]
     ids = iota((DATES, LIST), 0)
     signed = ((ids == refs).astype(F32) - (ids == secs).astype(F32)).astype(BF16)
@@ -207,61 +222,68 @@
     same = (held_in >> 6) == (held_out >> 6)
     row_in, row_out = (held_in >> 3) & 7, (held_out >> 3) & 7
     col_in, col_out = held_in & 7, held_out & 7
-    scale = edge_weight(row_out + p * MROWS, MROWS * GROUPS) * edge_weight(
-        col_out + s * MROWS, MROWS * STRIPES
+    row_keep = same & (col_in == col_out)
+    col_keep = same & (row_in == row_out)
+    for n in range(3):
+        shift = (n - 1) * MROWS
+        row_taps[n] = jnp.where(row_keep, tap(row_in + shift - row_out), 0.0)
+        far = col_in + s * MROWS + shift
+        col_ok = col_keep & (far >= 0) & (far < MROWS * STRIPES)
+        col_taps[n] = jnp.where(col_ok, tap(col_in + shift - col_out), 0.0)
+    held_row = (iota((8, 128), 1) >> 3) & 7
+    held_col = iota((8, 128), 1) & 7
+    scale[...] = 1.0 / (
+        edge_weight(held_row + p * MROWS, MROWS * GROUPS)
+        * edge_weight(held_col + s * MROWS, MROWS * STRIPES)
     )
-    for ci in range(3):
-        far = row_in + (p + ci - 1) * MROWS
-        near = row_out + p * MROWS
-        row_ok = same & (far >= 0) & (far < MROWS * GROUPS)
-        row_tap = jnp.where(row_ok, tap(far - near), 0.0)
-        for si in range(3):
-            far = col_in + (s + si - 1) * MROWS
-            near = col_out + s * MROWS
-            col_ok = (far >= 0) & (far < MROWS * STRIPES)
-            col_tap = jnp.where(col_ok, tap(far - near), 0.0)
-            weights[3 * ci + si] = row_tap * col_tap / scale
     total[...] = jnp.zeros(total.shape, F32)
 
     def lend(c):
         return pltpu.make_async_remote_copy(
-            src_ref=recv.at[c, pl.ds(0, AHEAD * TILE)],
-            dst_ref=recv.at[c, pl.ds(STRIPES * TILE, AHEAD * TILE)],
+            src_ref=recv.at[c, pl.ds(0, LENT)],
+            dst_ref=recv.at[c, pl.ds(STRIPES * TILE, LENT)],
             send_sem=lend_sem.at[c],
             recv_sem=borrow_sem.at[c],
             device_id=(lax.rem(p + GROUPS - 1, GROUPS), s),
             device_id_type=MESH,
         )
 
-    def part(c, ci, ds):
-        target = (c - ci + GROUPS) % GROUPS
+    def part(target, slot):
         rel = lax.rem(p - target + GROUPS, GROUPS)
-        slot = 3 * (ci + 1) + 1 - ds
-        source = right.at[c]
-        landing = blocks.at[slot, pl.ds(pl.multiple_of(rel * ROWS, 8), ROWS)]
-        remote = pltpu.make_async_remote_copy(
-            src_ref=source,
-            dst_ref=landing,
-            send_sem=part_send.at[c, slot],
+        ds = 0 if slot == 0 else 2 - slot
+        return pltpu.make_async_remote_copy(
+            src_ref=right.at[0 if slot == 0 else 1, target],
+            dst_ref=blocks.at[slot, pl.ds(pl.multiple_of(rel * ROWS, 8), ROWS)],
+            send_sem=part_send.at[target, slot],
             recv_sem=part_recv.at[rel, slot],
             device_id=(target, lax.rem(s + ds + STRIPES, STRIPES)),
             device_id_type=MESH,
         )
-        return target, slot, rel, remote
-
-    def chunk(c, carry):
-        def arrive(k, inner):
-            @pl.when(k != SELF)
-            def _():
-                arriving = stripe_copy(c, k)
-                arriving.wait_send()
-                arriving.wait_recv()
-
-            return inner
-
-        lax.fori_loop(0, STRIPES, arrive, 0)
-        lend(c).start()
-
+
+    def send_part(target, slot):
+        if slot in (1, 3):
+            part(target, slot).start()
+            return
+
+        @pl.when(p != target)
+        def _():
+            part(target, slot).start()
+
+        @pl.when(p == target)
+        def _():
+            blocks[slot, 0:ROWS, :] = right[0 if slot == 0 else 1, target]
+
+    def filter_rows(target):
+        filtered = jnp.zeros((ROWS, 128), F32)
+        for n in range(3):
+            c = target + n - 1
+            if 0 <= c < GROUPS:
+                filtered = filtered + dot(right[0, c], row_taps[n], HIGHEST)
+        right[1, target] = filtered
+        for slot in (1, 3, 2):
+            send_part(target, slot)
+
+    def products_of(c):
         def products(d, inner):
             base = pl.multiple_of(d * 64, 64)
 
@@ -275,61 +297,77 @@
                 real = jnp.sum(a * x + b * y, axis=0)
                 imag = jnp.sum(b * x - a * y, axis=0)
                 row = pl.multiple_of(((gap - 1) * BLOCK + d) * 16, 16)
-                acc[pl.ds(row, MROWS), :] = real
-                acc[pl.ds(row + MROWS, MROWS), :] = imag
+                acc[c % 2, pl.ds(row, MROWS), :] = real
+                acc[c % 2, pl.ds(row + MROWS, MROWS), :] = imag
             return inner
 
-        lax.fori_loop(0, BLOCK - GAPS, products, 0)
+        return products
+
+    def begin(c):
+        def first(n, inner):
+            @pl.when(s != n)
+            def _():
+                stripe_copy(c, turn_of(n)).wait_recv()
+
+            return inner
+
+        lax.fori_loop(0, 3, first, 0)
+        lend(c).start()
+        lax.fori_loop(3, STRIPES, first, 0)
+        lax.fori_loop(0, BLOCK - GAPS, products_of(c), 0)
+
+    def finish(c):
         lend(c).wait_recv()
-        lax.fori_loop(BLOCK - GAPS, BLOCK, products, 0)
-
+        lax.fori_loop(BLOCK - GAPS, BLOCK, products_of(c), 0)
         looked = jnp.zeros((COMBOS, 128), F32)
         lane = iota((2 * WIDTH, 128), 0) & (WIDTH - 1)
         column = iota((2 * WIDTH, 128), 1)
         for q in range(16):
-            summed = acc[pl.ds(q, COMBOS, stride=16), :]
+            summed = acc[c % 2, pl.ds(q, COMBOS, stride=16), :]
             high = summed.astype(BF16)
             low = (summed - high.astype(F32)).astype(BF16)
             pool = jnp.where(column == q * MROWS + (lane >> 4), 1.0 / 64.0, 0.0).astype(BF16)
             looked = looked + dot(jnp.concatenate([high, low], axis=1), pool)
-        right[c] = dot(design[...], looked.astype(BF16))
-        return carry
+        right[0, c] = dot(design[...], looked.astype(BF16))
+        send_part(c, 0)
+        if c > 0:
+            filter_rows(c - 1)
+        if c == GROUPS - 1:
+            filter_rows(c)
 
     for c in range(GROUPS):
-        chunk(c, 0)
-        for ci in (-1, 0, 1):
-            for ds in (-1, 0, 1):
-                target, slot, rel, remote = part(c, ci, ds)
-                if ds == 0:
-
-                    @pl.when(target != p)
-                    def _():
-                        remote.start()
-
-                    @pl.when(target == p)
-                    def _():
-                        blocks[slot, 0:ROWS, :] = right[c]
-                else:
-                    remote.start()
+        begin(c)
+        if c > 0:
+            finish(c - 1)
+    finish(GROUPS - 1)
+
+    for c in range(GROUPS):
         lend(c).wait_send()
 
-    for c in range(GROUPS):
-        for ci in (-1, 0, 1):
-            for ds in (-1, 0, 1):
-                target, slot, rel, remote = part(c, ci, ds)
-                if ds == 0:
-
-                    @pl.when(target != p)
-                    def _():
-                        remote.wait_send()
-                else:
-                    remote.wait_send()
+        def sent(k, carry, c=c):
+            @pl.when(k != SELF)
+            def _():
+                stripe_copy(c, k).wait_send()
+
+            return carry
+
+        lax.fori_loop(0, STRIPES, sent, 0)
+
+    for target in range(GROUPS):
+        for slot in (1, 3):
+            part(target, slot).wait_send()
+
+        @pl.when(p != target)
+        def _():
+            for slot in (0, 2):
+                part(target, slot).wait_send()
+
     for rel in range(GROUPS):
-        for slot in range(9):
-            if rel == 0 and slot % 3 == 1:
+        for slot in range(4):
+            if rel == 0 and slot in (0, 2):
                 continue
             pltpu.make_async_remote_copy(
-                src_ref=right.at[0],
+                src_ref=right.at[0, 0],
                 dst_ref=blocks.at[slot, pl.ds(rel * ROWS, ROWS)],
                 send_sem=part_send.at[0, slot],
                 recv_sem=part_recv.at[rel, slot],
@@ -337,10 +375,11 @@
                 device_id_type=MESH,
             ).wait_recv()
 
-    smooth = dot(blocks[0], weights[0], HIGHEST)
-    for slot in range(1, 9):
-        smooth = smooth + dot(blocks[slot], weights[slot], HIGHEST)
-    centre = blocks[4]
+    smooth = dot(blocks[1], col_taps[0], HIGHEST)
+    for n in range(1, 3):
+        smooth = smooth + dot(blocks[n + 1], col_taps[n], HIGHEST)
+    smooth = smooth * scale[0:1, :]
+    centre = blocks[0]
     for rel in range(GROUPS):
         group = lax.rem(p + rel, GROUPS)
         rows = pl.ds(pl.multiple_of(group * BLOCK, BLOCK), ROWS)
@@ -355,39 +394,44 @@
 
 def local(slc_stack, az_offset, rg_offset, pair_list):
     vmem = pl.BlockSpec(memory_space=pltpu.VMEM)
-    smem = pl.BlockSpec(memory_space=pltpu.SMEM)
     dma = pltpu.SemaphoreType.DMA
     result = jax.ShapeDtypeStruct((2 * MROWS * MROWS, DATES), F32)
     screen, motion = pl.pallas_call(
         kernel,
         out_shape=(result, result),
-        in_specs=[pl.BlockSpec(memory_space=pl.ANY), smem, smem, vmem],
+        in_specs=[pl.BlockSpec(memory_space=pltpu.HBM)] * 4,
         out_specs=(vmem, vmem),
         scratch_shapes=[
+            pltpu.SMEM((DATES,), jnp.int32),
+            pltpu.SMEM((DATES,), jnp.int32),
+            pltpu.VMEM((2, 1000), jnp.int32),
             pltpu.VMEM((2, 2 * LINES, RANGE + 2 * WIDTH), BF16),
             pltpu.VMEM((GROUPS, STRIPES, TILE, WIDTH), BF16),
-            pltpu.VMEM((GROUPS, (STRIPES + AHEAD) * TILE, WIDTH), BF16),
-            pltpu.VMEM((COMBOS * 16, WIDTH), F32),
+            pltpu.VMEM((GROUPS, STRIPES * TILE + LENT, WIDTH), BF16),
+            pltpu.VMEM((2, COMBOS * 16, WIDTH), F32),
             pltpu.VMEM((2, LINES, LINES), BF16),
             pltpu.VMEM((2, 3 * WIDTH, WIDTH), BF16),
             pltpu.VMEM((8, LIST), jnp.int32),
             pltpu.VMEM((DATES, DATES), F32),
             pltpu.VMEM((DATES, DATES), F32),
             pltpu.VMEM((ROWS, COMBOS), BF16),
-            pltpu.VMEM((9, 128, 128), F32),
-            pltpu.VMEM((GROUPS, ROWS, 128), F32),
-            pltpu.VMEM((9, GROUPS * ROWS, 128), F32),
+            pltpu.VMEM((3, 128, 128), F32),
+            pltpu.VMEM((3, 128, 128), F32),
+            pltpu.VMEM((8, 128), F32),
+            pltpu.VMEM((2, GROUPS, ROWS, 128), F32),
+            pltpu.VMEM((4, GROUPS * ROWS, 128), F32),
             pltpu.VMEM(((GROUPS - 1) * BLOCK + ROWS, 256), F32),
+            dma((3,)),
             dma((4,)),
             dma((GROUPS, STRIPES)),
             dma((GROUPS, STRIPES)),
             dma((GROUPS,)),
             dma((GROUPS,)),
-            dma((GROUPS, 9)),
-            dma((GROUPS, 9)),
+            dma((GROUPS, 4)),
+            dma((GROUPS, 4)),
         ],
         compiler_params=pltpu.CompilerParams(
-            collective_id=0, has_side_effects=True, vmem_limit_bytes=48 << 20
+            collective_id=0, has_side_effects=True, vmem_limit_bytes=(64 << 20) - (1 << 16)
         ),
     )(slc_stack, az_offset, rg_offset, pair_list.T)
 

time: 108 us -> 87.9 us (0.81); the launches traced: 107 us -> 87.8 us
  Pallas kernels: 100 us -> 84 us
  local copies, waits for them, and re-layouts: 5.55 us -> 3.14 us
    pallas_call x1, Pallas kernels: 100 us -> 84 us  [local(): pl.pallas_call(kernel, out_shape=(result, result), in_specs=[pl.BlockSpec...]
    unnamed x10 -> x2, local copies, waits for them, and re-layouts: 5.55 us -> 3.14 us
where the time goes in v2:
time: 87.9 us; the launch traced here: 87.8 us
  Pallas kernels  84 us (96%)
  local copies, waits for them, and re-layouts  3.14 us (4%)
    pallas_call x1, Pallas kernels, local(): pl.pallas_call(kernel, out_shape=(result, result), in_specs=[pl.BlockSpec...  84 us
    unnamed x2, local copies, waits for them, and re-layouts  3.14 us

profile of v2, /device:TPU:25, one launch (start us, length us, event | category | flops | bytes accessed | tf_op | source)
XLA Modules:
  0.0 87.8 jit_solution(7309721913068212423)
XLA Ops:
  0.6 84.0 %shard_map.59 = (f32[128,256]{1,0:T(8,128)}, f32[128,256]{1,0:T(8,128)}) custom-call(bf16[2,2,128,4096]{3,2,1,0:T(8,128)(2,1)} %slc.1, s32[256]{0:T(256)} %az_in.1, s32[256]{0:T(256)} %rg_in.1, s32[2,1000]{1,0:T(2,128)} %bitcast.9), custom_call_target="tpu_custom_call" | custom-call | tf_op jit(solution)/shard_map/pallas_call | solution.py:399
  84.7 1.6 %copy.8 = f32[256,2,8,8]{0,3,2,1:T(8,128)} copy(f32[256,2,8,8]{0,3,2,1:T(8,128)} %bitcast.8) | data formatting | bytes 262144
  86.2 1.6 %copy.9 = f32[256,2,8,8]{0,3,2,1:T(8,128)} copy(f32[256,2,8,8]{0,3,2,1:T(8,128)} %bitcast.7) | data formatting | bytes 262144

commit v3 on v2

--- a/solution.py
+++ b/solution.py
@@ -45,6 +45,21 @@
     )
 
 
+def split(value):
+    high = value.astype(BF16)
+    return high, (value - high.astype(F32)).astype(BF16)
+
+
+def stacked(value):
+    high, low = split(value)
+    return jnp.concatenate([high, high, low], axis=0)
+
+
+def dot_split(a, b):
+    high, low = split(a)
+    return dot(jnp.concatenate([high, low, high], axis=1), b)
+
+
 def dot_lanes(a, b):
     return lax.dot_general(a, b, (((1,), (1,)), ((), ())), preferred_element_type=F32)
 
@@ -74,8 +89,8 @@
 
 
 def kernel(
-    slc, az_in, rg_in, pairs_in, screen_out, motion_out,
-    az, rg, listed, image, send, recv, acc, smap, rmap, plist, normal, inverse, design, row_taps, col_taps, scale,
+    slc, az_in, rg_in, pairs_in, solved_out,
+    az, rg, listed, image, send, recv, acc, smap, rmap, plist, normal, inverse, design, row_taps, col_taps, scale, pool, solver,
     right, blocks, total, small_sem, image_sem, send_sem, recv_sem, lend_sem, borrow_sem, part_send, part_recv,
 ):
     p = lax.axis_index("pairs")
@@ -205,6 +220,7 @@
         return carry
 
     lax.fori_loop(0, NEWTON, newton, 0)
+    solver[...] = stacked(inverse[...])
 
     local = refs - p * BLOCK
     inside = (local >= 0) & (local < BLOCK)
@@ -226,10 +242,10 @@
     col_keep = same & (row_in == row_out)
     for n in range(3):
         shift = (n - 1) * MROWS
-        row_taps[n] = jnp.where(row_keep, tap(row_in + shift - row_out), 0.0)
+        row_taps[n] = stacked(jnp.where(row_keep, tap(row_in + shift - row_out), 0.0))
         far = col_in + s * MROWS + shift
         col_ok = col_keep & (far >= 0) & (far < MROWS * STRIPES)
-        col_taps[n] = jnp.where(col_ok, tap(col_in + shift - col_out), 0.0)
+        col_taps[n] = stacked(jnp.where(col_ok, tap(col_in + shift - col_out), 0.0))
     held_row = (iota((8, 128), 1) >> 3) & 7
     held_col = iota((8, 128), 1) & 7
     scale[...] = 1.0 / (
@@ -237,6 +253,11 @@
         * edge_weight(held_col + s * MROWS, MROWS * STRIPES)
     )
     total[...] = jnp.zeros(total.shape, F32)
+    lane = iota((2 * WIDTH, 128), 0) & (WIDTH - 1)
+    column = iota((2 * WIDTH, 128), 1)
+    for u in range(MROWS):
+        hit = column == ((lane >> 3) & 1) * 64 + u * MROWS + (lane >> 4)
+        pool[pl.ds(u * 2 * WIDTH, 2 * WIDTH), :] = jnp.where(hit, 1.0 / 64.0, 0.0).astype(BF16)
 
     def lend(c):
         return pltpu.make_async_remote_copy(
@@ -278,7 +299,7 @@
         for n in range(3):
             c = target + n - 1
             if 0 <= c < GROUPS:
-                filtered = filtered + dot(right[0, c], row_taps[n], HIGHEST)
+                filtered = filtered + dot_split(right[0, c], row_taps[n])
         right[1, target] = filtered
         for slot in (1, 3, 2):
             send_part(target, slot)
@@ -314,20 +335,20 @@
         lax.fori_loop(0, 3, first, 0)
         lend(c).start()
         lax.fori_loop(3, STRIPES, first, 0)
-        lax.fori_loop(0, BLOCK - GAPS, products_of(c), 0)
+        lax.fori_loop(0, BLOCK - GAPS - 1, products_of(c), 0, unroll=2)
 
     def finish(c):
         lend(c).wait_recv()
-        lax.fori_loop(BLOCK - GAPS, BLOCK, products_of(c), 0)
-        looked = jnp.zeros((COMBOS, 128), F32)
-        lane = iota((2 * WIDTH, 128), 0) & (WIDTH - 1)
-        column = iota((2 * WIDTH, 128), 1)
-        for q in range(16):
-            summed = acc[c % 2, pl.ds(q, COMBOS, stride=16), :]
-            high = summed.astype(BF16)
-            low = (summed - high.astype(F32)).astype(BF16)
-            pool = jnp.where(column == q * MROWS + (lane >> 4), 1.0 / 64.0, 0.0).astype(BF16)
-            looked = looked + dot(jnp.concatenate([high, low], axis=1), pool)
+        lax.fori_loop(BLOCK - GAPS - 1, BLOCK, products_of(c), 0, unroll=2)
+        front = (iota((COMBOS, WIDTH), 1) & 8) == 0
+        cut = []
+        for u in range(MROWS):
+            real = acc[c % 2, pl.ds(u, COMBOS, stride=16), :]
+            imag = acc[c % 2, pl.ds(u + MROWS, COMBOS, stride=16), :]
+            real = real + pltpu.roll(real, WIDTH - 8, 1)
+            imag = imag + pltpu.roll(imag, 8, 1)
+            cut.extend(split(jnp.where(front, real, imag)))
+        looked = dot(jnp.concatenate(cut, axis=1), pool[...])
         right[0, c] = dot(design[...], looked.astype(BF16))
         send_part(c, 0)
         if c > 0:
@@ -375,9 +396,9 @@
                 device_id_type=MESH,
             ).wait_recv()
 
-    smooth = dot(blocks[1], col_taps[0], HIGHEST)
+    smooth = dot_split(blocks[1], col_taps[0])
     for n in range(1, 3):
-        smooth = smooth + dot(blocks[n + 1], col_taps[n], HIGHEST)
+        smooth = smooth + dot_split(blocks[n + 1], col_taps[n])
     smooth = smooth * scale[0:1, :]
     centre = blocks[0]
     for rel in range(GROUPS):
@@ -386,21 +407,20 @@
         cut = slice(rel * ROWS, (rel + 1) * ROWS)
         total[rows, 0:128] = total[rows, 0:128] + centre[cut]
         total[rows, 128:256] = total[rows, 128:256] + smooth[cut]
-    solved = dot(inverse[...], total[0:DATES, :], HIGHEST)
-    screen = solved[:, 128:256]
-    screen_out[...] = screen.T
-    motion_out[...] = (solved[:, 0:128] - screen).T
+    high, low = split(total[0:DATES, :])
+    solved = dot(
+        jnp.concatenate([high.T, low.T, high.T], axis=1), solver[...]
+    )
+    solved_out[...] = solved
 
 
 def local(slc_stack, az_offset, rg_offset, pair_list):
-    vmem = pl.BlockSpec(memory_space=pltpu.VMEM)
     dma = pltpu.SemaphoreType.DMA
-    result = jax.ShapeDtypeStruct((2 * MROWS * MROWS, DATES), F32)
-    screen, motion = pl.pallas_call(
+    solved = pl.pallas_call(
         kernel,
-        out_shape=(result, result),
+        out_shape=jax.ShapeDtypeStruct((2 * 2 * MROWS * MROWS, DATES), F32),
         in_specs=[pl.BlockSpec(memory_space=pltpu.HBM)] * 4,
-        out_specs=(vmem, vmem),
+        out_specs=pl.BlockSpec(memory_space=pltpu.VMEM),
         scratch_shapes=[
             pltpu.SMEM((DATES,), jnp.int32),
             pltpu.SMEM((DATES,), jnp.int32),
@@ -415,9 +435,11 @@
             pltpu.VMEM((DATES, DATES), F32),
             pltpu.VMEM((DATES, DATES), F32),
             pltpu.VMEM((ROWS, COMBOS), BF16),
-            pltpu.VMEM((3, 128, 128), F32),
-            pltpu.VMEM((3, 128, 128), F32),
+            pltpu.VMEM((3, 384, 128), BF16),
+            pltpu.VMEM((3, 384, 128), BF16),
             pltpu.VMEM((8, 128), F32),
+            pltpu.VMEM((MROWS * 2 * WIDTH, 128), BF16),
+            pltpu.VMEM((3 * DATES, DATES), BF16),
             pltpu.VMEM((2, GROUPS, ROWS, 128), F32),
             pltpu.VMEM((4, GROUPS * ROWS, 128), F32),
             pltpu.VMEM(((GROUPS - 1) * BLOCK + ROWS, 256), F32),
@@ -438,7 +460,8 @@
     def placed(value):
         return value.reshape(2, MROWS, MROWS, DATES).transpose(3, 0, 1, 2)
 
-    return placed(screen), placed(motion)
+    series, screen = solved[:128], solved[128:]
+    return placed(screen), placed(series - screen)
 
 
 def solution(mesh):

time: 87.9 us -> 82.7 us (0.941)
  Pallas kernels: 84 us -> 80.2 us
  local copies, waits for them, and re-layouts: 3.14 us -> 0 us
  other arithmetic: 0 us -> 1.69 us
    pallas_call x1, Pallas kernels: 84 us -> 80.2 us  [local(): pl.pallas_call(kernel, out_shape=jax.ShapeDtypeStruct((2 * 2 * MROWS * MR...]
    unnamed x2 -> x0, local copies, waits for them, and re-layouts: 3.14 us -> none
    sub x0 -> x1, other arithmetic: none -> 1.69 us  [local(): return (placed(screen), placed(series - screen))]
where the time goes in v3:
time: 82.7 us; the launch traced here: 82.5 us
  Pallas kernels  80.2 us (97%)
  other arithmetic  1.69 us (2%)
    pallas_call x1, Pallas kernels, local(): pl.pallas_call(kernel, out_shape=jax.ShapeDtypeStruct((2 * 2 * MROWS * MR...  80.2 us
    sub x1, other arithmetic, local(): return (placed(screen), placed(series - screen))  1.69 us

profile of v3, /device:TPU:25, one launch (start us, length us, event | category | flops | bytes accessed | tf_op | source)
XLA Modules:
  0.0 82.5 jit_solution(16337736411946712270)
XLA Ops:
  0.6 80.2 %shard_map.59 = f32[256,256]{1,0:T(8,128)} custom-call(bf16[2,2,128,4096]{3,2,1,0:T(8,128)(2,1)} %slc.1, s32[256]{0:T(256)} %az_in.1, s32[256]{0:T(256)} %rg_in.1, s32[2,1000]{1,0:T(2,128)} %bitcast.9), custom_call_target="tpu_custom_call" | custom-call | tf_op jit(solution)/shard_map/pallas_call | solution.py:419
  80.8 1.7 %slice_subtract_fusion = (f32[128,256]{1,0:T(8,128)}, f32[128,256]{1,0:T(8,128)}) fusion(f32[256,256]{1,0:T(8,128)} %shard_map.59), kind=kLoop, calls=%fused_computation | loop fusion | flops 32768 | bytes 524288 | tf_op jit(solution)/shard_map/sub | solution.py:464

commit v4 on v3

--- a/solution.py
+++ b/solution.py
@@ -163,8 +163,8 @@
         return pltpu.make_async_remote_copy(
             src_ref=send.at[c, target],
             dst_ref=recv.at[c, pl.ds(s * TILE, TILE)],
-            send_sem=send_sem.at[c, k],
-            recv_sem=recv_sem.at[c, k],
+            send_sem=send_sem.at[c],
+            recv_sem=recv_sem.at[c],
             device_id=(p, target),
             device_id_type=MESH,
         )
@@ -325,16 +325,16 @@
         return products
 
     def begin(c):
-        def first(n, inner):
-            @pl.when(s != n)
-            def _():
-                stripe_copy(c, turn_of(n)).wait_recv()
-
-            return inner
-
-        lax.fori_loop(0, 3, first, 0)
+        arrived = send.at[c, pl.ds(0, STRIPES - 1)]
+        pltpu.make_async_remote_copy(
+            src_ref=arrived,
+            dst_ref=arrived,
+            send_sem=send_sem.at[c],
+            recv_sem=recv_sem.at[c],
+            device_id=(p, peer(0)),
+            device_id_type=MESH,
+        ).wait_recv()
         lend(c).start()
-        lax.fori_loop(3, STRIPES, first, 0)
         lax.fori_loop(0, BLOCK - GAPS - 1, products_of(c), 0, unroll=2)
 
     def finish(c):
@@ -365,14 +365,15 @@
     for c in range(GROUPS):
         lend(c).wait_send()
 
-        def sent(k, carry, c=c):
-            @pl.when(k != SELF)
-            def _():
-                stripe_copy(c, k).wait_send()
-
-            return carry
-
-        lax.fori_loop(0, STRIPES, sent, 0)
+        all_sent = send.at[c, pl.ds(0, STRIPES - 1)]
+        pltpu.make_async_remote_copy(
+            src_ref=all_sent,
+            dst_ref=all_sent,
+            send_sem=send_sem.at[c],
+            recv_sem=recv_sem.at[c],
+            device_id=(p, peer(0)),
+            device_id_type=MESH,
+        ).wait_send()
 
     for target in range(GROUPS):
         for slot in (1, 3):
@@ -445,8 +446,8 @@
             pltpu.VMEM(((GROUPS - 1) * BLOCK + ROWS, 256), F32),
             dma((3,)),
             dma((4,)),
-            dma((GROUPS, STRIPES)),
-            dma((GROUPS, STRIPES)),
+            dma((GROUPS,)),
+            dma((GROUPS,)),
             dma((GROUPS,)),
             dma((GROUPS,)),
             dma((GROUPS, 4)),

time: 82.7 us -> 79.8 us (0.965)
  the two profiles are of different devices: /device:TPU:25 before, /device:TPU:17 now
where the time goes in v4:
time: 79.8 us; the launch traced here: 79.7 us
  Pallas kernels  77.3 us (97%)
  other arithmetic  1.69 us (2%)
    pallas_call x1, Pallas kernels, local(): pl.pallas_call(kernel, out_shape=jax.ShapeDtypeStruct((2 * 2 * MROWS * MR...  77.3 us
    sub x1, other arithmetic, local(): return (placed(screen), placed(series - screen))  1.69 us

profile of v4, /device:TPU:17, one launch (start us, length us, event | category | flops | bytes accessed | tf_op | source)
XLA Modules:
  0.0 79.7 jit_solution(7566475389685406232)
XLA Ops:
  0.6 77.3 %shard_map.59 = f32[256,256]{1,0:T(8,128)} custom-call(bf16[2,2,128,4096]{3,2,1,0:T(8,128)(2,1)} %slc.1, s32[256]{0:T(256)} %az_in.1, s32[256]{0:T(256)} %rg_in.1, s32[2,1000]{1,0:T(2,128)} %bitcast.9), custom_call_target="tpu_custom_call" | custom-call | tf_op jit(solution)/shard_map/pallas_call | solution.py:420
  78.0 1.7 %slice_subtract_fusion = (f32[128,256]{1,0:T(8,128)}, f32[128,256]{1,0:T(8,128)}) fusion(f32[256,256]{1,0:T(8,128)} %shard_map.59), kind=kLoop, calls=%fused_computation | loop fusion | flops 32768 | bytes 524288 | tf_op jit(solution)/shard_map/sub | solution.py:465
